TPU v7x, 512 devices: a whole 4x8x8 slice. The times are simulated.
512 devices in a mesh: dp: 8 (over x, core), ctx: 64 (over y, z).
Axes of the slice: x: 4, y: 8, z: 8, core: 2. Of those that a mesh axis runs over, the one named last changes fastest.
Arguments:
- queries: bfloat16 [8192, 4096], P(('dp', 'ctx')), may hold values from -150 to 150
- keys: bfloat16 [131072, 1024], P(('dp', 'ctx')), may hold values from -8 to 8
- values: bfloat16 [131072, 1024], P(('dp', 'ctx')), may hold values from -6 to 6
- learned_compress_queries: bfloat16 [16, 1024], replicated, may hold values from -150 to 150
- span_len: int32 [8, 64], P('dp', 'ctx'), may hold values from 1 to 16, 768 in all within a row
- span_offset: int32 [8, 64], P('dp', 'ctx'), may hold values from 0 to 240
- destination: int32 [8192, 1], P(('dp', 'ctx')), may hold values from 0 to 63; in each aligned block of 16 rows (0 to 15, 16 to 31, ...) at most 2 rows name the same one
- cotangent: bfloat16 [8192, 4096], P(('dp', 'ctx')), may hold values from -6 to 6
- adapter_a: bfloat16 [64, 16, 4096], P('ctx'), may hold values from -0.09375 to 0.09375
- adapter_b: bfloat16 [64, 16, 4096], P('ctx'), may hold values from -0.09375 to 0.09375
Outputs:
- grad_rows: bfloat16 [8192, 4096], P(('dp', 'ctx'))
- grad_a: float32 [64, 16, 4096], P('ctx')
- grad_b: float32 [64, 16, 4096], P('ctx')
Inputs may be any that keep to these rules, and one draw needn't show every extreme that they name: `destination`: in each device's 16 slots (aligned blocks of rows) no decoder is named more than 2 times, a bound that some block reaches.
All inputs are finite; a program needn't handle non-finite values. No bound on the sum of `span_len` on one device may be relied on, other than what follows from the above.
Results may differ from a plain program's by a relative error of at most 0.025.
Values may be sent and summed in bfloat16 or wider, within the bound.
A program may use at most 64 MiB of HBM per device.

v0:
```python
import math
import jax
import jax.numpy as jnp
from jax import lax
from jax.sharding import PartitionSpec as P

QUERY_HEADS = 32
KEY_VALUE_HEADS = 8
HEAD_SIZE = 128
COMPRESSED_ROWS = 16
SCALE = 2.0
EPS = 1e-06
NEGATIVE_FLOOR = -1e30


def absorb(state, query_matrix, keys_blk, vals_blk, visible):
    count = keys_blk.shape[0]
    heads = query_matrix.shape[1]
    width = query_matrix.shape[3]
    expanded_keys = keys_blk.reshape(count, heads, width)
    expanded_values = vals_blk.reshape(count, heads, width)
    attention_score = jnp.einsum(
        "shgd,nhd->shgn", query_matrix, expanded_keys, preferred_element_type=jnp.float32
    ) * (1.0 / math.sqrt(width))
    seen = visible[:, None, None, :]
    attention_score = jnp.where(seen, attention_score, NEGATIVE_FLOOR)
    peak, total, accum = state
    newpeak = jnp.maximum(peak, jnp.max(attention_score, axis=-1))
    keep = jnp.exp(peak - newpeak)
    prob = jnp.where(seen, jnp.exp(attention_score - newpeak[..., None]), 0.0)
    total = total * keep + jnp.sum(prob, axis=-1)
    accum = accum * keep[..., None] + jnp.einsum(
        "shgn,nhd->shgd",
        prob.astype(jnp.bfloat16),
        expanded_values,
        preferred_element_type=jnp.float32,
    )
    return (newpeak, total, accum)


def absorb_rows(state, query_matrix, keys_blk, vals_blk, visible):
    count = keys_blk.shape[0]
    blocks = count // 256
    kb = keys_blk.reshape(blocks, 256, keys_blk.shape[1])
    vb = vals_blk.reshape(blocks, 256, vals_blk.shape[1])
    mb = visible.reshape(visible.shape[0], blocks, 256).transpose(1, 0, 2)

    def step(current, item):
        return (absorb(current, query_matrix, item[0], item[1], item[2]), None)

    state, _ = lax.scan(step, state, (kb, vb, mb))
    return state


def attend(queries, keys, values, learned_compress_queries, offset, length):
    span_slots = queries.shape[0]
    model = queries.shape[1]
    segment_length = keys.shape[0]
    query_group = QUERY_HEADS // KEY_VALUE_HEADS
    here = lax.axis_index("ctx")
    query_matrix = queries.reshape(span_slots, KEY_VALUE_HEADS, query_group, HEAD_SIZE)
    expanded_keys = keys.reshape(segment_length, KEY_VALUE_HEADS, HEAD_SIZE)
    expanded_values = values.reshape(segment_length, KEY_VALUE_HEADS, HEAD_SIZE)
    compressor_query = learned_compress_queries.reshape(COMPRESSED_ROWS, KEY_VALUE_HEADS, HEAD_SIZE)
    attention_score = jnp.einsum(
        "cpf,ipf->pci", compressor_query, expanded_keys, preferred_element_type=jnp.float32
    ) * (1.0 / math.sqrt(HEAD_SIZE))
    softmax_weight = jax.nn.softmax(attention_score, axis=-1).astype(jnp.bfloat16)
    short_keys = (
        jnp.einsum(
            "wio,owx->iwx", softmax_weight, expanded_keys, preferred_element_type=jnp.float32
        )
        .astype(jnp.bfloat16)
        .reshape(COMPRESSED_ROWS, KEY_VALUE_HEADS * HEAD_SIZE)
    )
    short_vals = (
        jnp.einsum(
            "wio,owx->iwx", softmax_weight, expanded_values, preferred_element_type=jnp.float32
        )
        .astype(jnp.bfloat16)
        .reshape(COMPRESSED_ROWS, KEY_VALUE_HEADS * HEAD_SIZE)
    )
    state = (
        jnp.full((span_slots, KEY_VALUE_HEADS, query_group), NEGATIVE_FLOOR, jnp.float32),
        jnp.zeros((span_slots, KEY_VALUE_HEADS, query_group), jnp.float32),
        jnp.zeros((span_slots, KEY_VALUE_HEADS, query_group, HEAD_SIZE), jnp.float32),
    )
    position = offset + jnp.arange(span_slots, dtype=jnp.int32)
    local = jnp.arange(segment_length, dtype=jnp.int32)[None, :] <= position[:, None]
    state = absorb(state, query_matrix, keys, values, local)
    piece = (
        lax.all_gather(short_keys, "ctx", axis=0, tiled=True),
        lax.all_gather(short_vals, "ctx", axis=0, tiled=True),
    )
    count = piece[0].shape[0]
    source = jnp.arange(count, dtype=jnp.int32) // COMPRESSED_ROWS
    state = absorb_rows(state, query_matrix, piece[0], piece[1], (source < here)[None, :])
    peak, total, accum = state
    out = (accum / total[..., None]).reshape(span_slots, model)
    live = (jnp.arange(span_slots, dtype=jnp.int32) < length)[:, None]
    return jnp.where(live, out, 0.0).astype(jnp.bfloat16)


def shards(
    queries,
    keys,
    values,
    learned_compress_queries,
    span_len,
    span_offset,
    destination,
    cotangent,
    adapter_a,
    adapter_b,
):
    span_slots = queries.shape[0]
    model = queries.shape[1]
    count = lax.axis_size("ctx")
    cap = max(2, (3 * span_slots + 2 * count - 1) // (2 * count))
    offset = span_offset[0, 0]
    length = span_len[0, 0]
    live = (jnp.arange(span_slots, dtype=jnp.int32) < length)[:, None]
    dy = jnp.where(live, cotangent, jnp.zeros_like(cotangent))
    target = destination[:, 0]
    order_idx = jnp.arange(span_slots, dtype=jnp.int32)
    same = target[:, None] == target[None, :]
    before = order_idx[None, :] < order_idx[:, None]
    rank = jnp.sum((same & before).astype(jnp.int32), axis=1)
    slot = target * cap + rank
    place = (jnp.arange(count * cap, dtype=jnp.int32)[:, None] == slot[None, :]).astype(
        jnp.bfloat16
    )

    def packed(row_block):
        return (
            jnp.dot(place, row_block, preferred_element_type=jnp.float32)
            .astype(jnp.bfloat16)
            .reshape(count, cap, model)
        )

    attn = attend(queries, keys, values, learned_compress_queries, offset, length)
    rows_in, dy_in = (
        lax.all_to_all(packed(attn), "ctx", split_axis=0, concat_axis=0, tiled=True),
        lax.all_to_all(packed(dy), "ctx", split_axis=0, concat_axis=0, tiled=True),
    )
    x = rows_in.reshape(count * cap, model).astype(jnp.float32)
    grads_in = dy_in.reshape(count * cap, model)
    rs = lax.rsqrt(jnp.mean(x * x, axis=-1, keepdims=True) + EPS)
    nrm = x * rs
    normed = nrm.astype(jnp.bfloat16)
    down = adapter_a[0]
    upper = adapter_b[0]
    across = (((1,), (1,)), ((), ()))
    along = (((0,), (0,)), ((), ()))
    hid = lax.dot_general(normed, down, across, preferred_element_type=jnp.float32).astype(
        jnp.bfloat16
    )
    back = (
        SCALE * lax.dot_general(grads_in, upper, across, preferred_element_type=jnp.float32)
    ).astype(jnp.bfloat16)
    grad_b = SCALE * lax.dot_general(hid, grads_in, along, preferred_element_type=jnp.float32)
    grad_a = lax.dot_general(back, normed, along, preferred_element_type=jnp.float32)
    dn = jnp.dot(back, down, preferred_element_type=jnp.float32)
    d_rows = (
        grads_in.astype(jnp.float32) + rs * (dn - nrm * jnp.mean(dn * nrm, axis=-1, keepdims=True))
    ).astype(jnp.bfloat16)
    returned = lax.all_to_all(
        d_rows.reshape(count, cap, model), "ctx", split_axis=0, concat_axis=0, tiled=True
    )
    grad_rows = lax.dot_general(
        place, returned.reshape(count * cap, model), along, preferred_element_type=jnp.float32
    ).astype(jnp.bfloat16)
    grad_a, grad_b = (
        lax.psum(grad_a.astype(jnp.bfloat16), "dp").astype(jnp.float32),
        lax.psum(grad_b.astype(jnp.bfloat16), "dp").astype(jnp.float32),
    )
    return (grad_rows, grad_a[None], grad_b[None])


def solution(mesh):
    in_specs = (
        P(("dp", "ctx"), None),
        P(("dp", "ctx"), None),
        P(("dp", "ctx"), None),
        P(),
        P("dp", "ctx"),
        P("dp", "ctx"),
        P(("dp", "ctx"), None),
        P(("dp", "ctx"), None),
        P("ctx", None, None),
        P("ctx", None, None),
    )
    out_specs = (P(("dp", "ctx"), None), P("ctx", None, None), P("ctx", None, None))
    return jax.shard_map(shards, mesh=mesh, in_specs=in_specs, out_specs=out_specs, check_vma=False)
```

profile of v0, /device:TPU:8, one launch (start us, length us, event | category | flops | bytes accessed | tf_op | source)
XLA Modules:
  0.0 355.6 jit_solution(18318135870249494899)
XLA Ops:
  7.2 1.5 fusion.61
  8.8 1.3 fusion.19
  10.8 1.3 fusion.20
  14.1 1.5 reshape.203
  15.6 16.9 %all-to-all-start = ((bf16[64,2,4096]{2,1,0:T(2,128)(2,1)}), bf16[64,2,4096]{2,1,0:T(2,128)(2,1)}, u32[]{:S(2)}, u32[]{:S(2)}) async-start(bf16[64,2,4096]{2,1,0:T(2,128)(2,1)} %reshape.203), calls=%async_computation | async-start | bytes 2097152 | tf_op jit(solution)/shard_map/all_to_all | solution.py:144
  34.6 82.2 %all-gather.3.cloned.1.call-done = bf16[1024,1024]{1,0:T(8,128)(2,1)} async-done(((bf16[16,1024]{1,0:T(8,128)(2,1)}), bf16[1024,1024]{1,0:T(8,128)(2,1)}) %all-gather.3.cloned.1.call-update) | async-done | bytes 2097168 | tf_op jit(solution)/shard_map/all_gather | solution.py:92
  116.9 84.1 %all-gather.5.cloned.1.call-done = bf16[1024,1024]{1,0:T(8,128)(2,1)} async-done(((bf16[16,1024]{1,0:T(8,128)(2,1)}), bf16[1024,1024]{1,0:T(8,128)(2,1)}) %all-gather.5.cloned.1.call-update) | async-done | bytes 2097168 | tf_op jit(solution)/shard_map/all_gather | solution.py:93
  201.0 11.0 %while.14 = (s32[]{:T(128)}, f32[16,8,4]{0,2,1:T(4,128)S(1)}, f32[16,8,4]{0,2,1:T(4,128)S(1)}, f32[16,8,4,128]{3,0,2,1:T(8,128)S(1)}, pred[4,1,256]{2,1,0:T(4,12...) while((s32[]{:T(128)}, f32[16,8,4]{0,2,1:T(4,128)S(1)}, ...), condition=%wide.region_8.9_spmd, body=%wide.region_5.8_spmd.sunk | while | flops 68420608 | bytes 7505253 | solution.py:51
  203.8 1.3 constant_dynamic-slice_fusion.3
  206.5 1.3 constant_dynamic-slice_fusion.3
  212.8 1.5 reshape.214
  214.3 9.5 %all-to-all-start.1 = ((bf16[64,2,4096]{2,1,0:T(2,128)(2,1)}), bf16[64,2,4096]{2,1,0:T(2,128)(2,1)S(1)}, u32[]{:S(2)}, u32[]{:S(2)}) async-start(bf16[64,2,4096]{2,1,0:T(2,128)(2,1)} %reshape.214), calls=%async_computation.1 | async-start | bytes 2097152 | tf_op jit(solution)/shard_map/all_to_all | solution.py:143
  223.8 1.5 reshape.204
  225.7 23.5 %all-to-all-done.1 = bf16[64,2,4096]{2,1,0:T(2,128)(2,1)S(1)} async-done(((bf16[64,2,4096]{2,1,0:T(2,128)(2,1)}), bf16[64,2,4096]{2,1,0:T(2,128)(2,1)S(1)}, u32[]{:S(2)}, u32[]{:S(2)}) %all-to-all-start.1) | async-done | bytes 1048608 | tf_op jit(solution)/shard_map/all_to_all | solution.py:143
  252.1 1.7 add_convert_fusion
  253.8 2.5 reshape.215
  256.3 6.9 %all-to-all-start.2 = ((bf16[64,2,4096]{2,1,0:T(2,128)(2,1)}), bf16[64,2,4096]{2,1,0:T(2,128)(2,1)}, u32[]{:S(2)}, u32[]{:S(2)}) async-start(bf16[64,2,4096]{2,1,0:T(2,128)(2,1)} %reshape.215), calls=%async_computation.2 | async-start | bytes 2097152 | tf_op jit(solution)/shard_map/all_to_all | solution.py:167
  263.4 2.4 multiply_convert_fusion
  265.8 2.3 convert_element_type.95
  269.1 2.8 fusion.13
  271.9 71.4 %all-reduce.3.cloned.1.call-done = (bf16[1,16,4096]{2,1,0:T(8,128)(2,1)}, bf16[1,16,4096]{2,1,0:T(8,128)(2,1)}) async-done(((bf16[1,16,4096]{2,1,0:T(8,128)(2,1)}, bf16[1,16,4096]{2,1,0:T(8,128)(2,1)}), (bf16[1,16,4096]{2,1,0:T(8,128)(2,1)}, bf16[1,16,4096]{2,1,0:T(8,128)(2,1)})) %all-reduce.3.cloned.1.call-update) | async-done | bytes 262160 | tf_op jit(solution)/shard_map/psum | solution.py:174
  343.4 1.6 broadcast_in_dim.108
  345.0 1.6 broadcast_in_dim.110
  346.6 1.5 reshape.216
  (97 shorter events, 17.9 us)
Async XLA Ops:
  7.2 243.7 %copy-start = (bf16[1,16,4096]{2,1,0:T(8,128)(2,1)S(1)}, bf16[1,16,4096]{2,1,0:T(8,128)(2,1)}, u32[]{:S(2)}) copy-start(bf16[1,16,4096]{2,1,0:T(8,128)(2,1)} %param.20) | copy-start | bytes 393220
  7.2 6.2 %copy-start.9 = (s32[16,1]{0,1:T(1,128)S(1)}, s32[16,1]{0,1:T(1,128)}, u32[]{:S(2)}) copy-start(s32[16,1]{0,1:T(1,128)} %param.18) | copy-start | bytes 196
  7.2 6.4 %copy-start.8 = (bf16[16,4096]{1,0:T(8,128)(2,1)S(1)}, bf16[16,4096]{1,0:T(8,128)(2,1)}, u32[]{:S(2)}) copy-start(bf16[16,4096]{1,0:T(8,128)(2,1)} %param.19) | copy-start | bytes 393220
  7.2 109.7 %all-gather.3.cloned.1.call-start = ((), (), s32[]{:S(2)}) async-start(), calls=%async_computation.3 | async-start | bytes 2129920 | tf_op jit(solution)/shard_map/all_gather | solution.py:92
  10.7 190.3 %all-gather.5.cloned.1.call-start = ((), (), s32[]{:S(2)}) async-start(), calls=%async_computation.4 | async-start | bytes 2129920 | tf_op jit(solution)/shard_map/all_gather | solution.py:93
  14.0 19.1 %copy-start.7 = (bf16[16,4096]{1,0:T(8,128)(2,1)S(1)}, bf16[16,4096]{1,0:T(8,128)(2,1)}, u32[]{:S(2)}) copy-start(bf16[16,4096]{1,0:T(8,128)(2,1)} %param.12) | copy-start | bytes 393220
  14.1 19.2 %copy-start.4 = (bf16[256,1024]{1,0:T(8,128)(2,1)S(1)}, bf16[256,1024]{1,0:T(8,128)(2,1)}, u32[]{:S(2)}) copy-start(bf16[256,1024]{1,0:T(8,128)(2,1)} %param.13) | copy-start | bytes 1572868
  15.6 17.8 %copy-start.5 = (bf16[256,1024]{1,0:T(8,128)(2,1)S(1)}, bf16[256,1024]{1,0:T(8,128)(2,1)}, u32[]{:S(2)}) copy-start(bf16[256,1024]{1,0:T(8,128)(2,1)} %param.14) | copy-start | bytes 1572868
  15.6 198.7 %all-to-all-start = ((bf16[64,2,4096]{2,1,0:T(2,128)(2,1)}), bf16[64,2,4096]{2,1,0:T(2,128)(2,1)}, u32[]{:S(2)}, u32[]{:S(2)}) async-start(bf16[64,2,4096]{2,1,0:T(2,128)(2,1)} %reshape.203), calls=%async_computation | async-start | bytes 2097152 | tf_op jit(solution)/shard_map/all_to_all | solution.py:144
  214.3 11.0 %copy-start.6 = (bf16[1,16,4096]{2,1,0:T(8,128)(2,1)S(1)}, bf16[1,16,4096]{2,1,0:T(8,128)(2,1)}, u32[]{:S(2)}) copy-start(bf16[1,16,4096]{2,1,0:T(8,128)(2,1)} %param.21) | copy-start | bytes 393220
  214.3 34.9 %all-to-all-start.1 = ((bf16[64,2,4096]{2,1,0:T(2,128)(2,1)}), bf16[64,2,4096]{2,1,0:T(2,128)(2,1)S(1)}, u32[]{:S(2)}, u32[]{:S(2)}) async-start(bf16[64,2,4096]{2,1,0:T(2,128)(2,1)} %reshape.214), calls=%async_computation.1 | async-start | bytes 2097152 | tf_op jit(solution)/shard_map/all_to_all | solution.py:143
  225.3 25.1 %copy-start.1 = (bf16[128,4096]{1,0:T(8,128)(2,1)}, bf16[128,4096]{1,0:T(8,128)(2,1)S(1)}, u32[]{:S(2)}) copy-start(bf16[128,4096]{1,0:T(8,128)(2,1)S(1)} %reshape.204) | copy-start | bytes 3145732
  250.9 1.2 copy-start.2
  256.3 90.3 %all-to-all-start.2 = ((bf16[64,2,4096]{2,1,0:T(2,128)(2,1)}), bf16[64,2,4096]{2,1,0:T(2,128)(2,1)}, u32[]{:S(2)}, u32[]{:S(2)}) async-start(bf16[64,2,4096]{2,1,0:T(2,128)(2,1)} %reshape.215), calls=%async_computation.2 | async-start | bytes 2097152 | tf_op jit(solution)/shard_map/all_to_all | solution.py:167
  263.2 80.2 %all-reduce.3.cloned.1.call-start = ((), (), s32[]{:S(2)}) async-start(), calls=%async_computation.5 | async-start | bytes 524288 | tf_op jit(solution)/shard_map/psum | solution.py:174
  265.8 3.3 copy-start.3
Sparse Core Ops, SparseCore 0:
  11.6 105.2 all-gather.2
  120.5 80.5 all-gather.4
  272.1 71.2 all-reduce.2
where the time goes:
time: 356 us
  waiting for transfers between devices  261 us (73%)
  starting transfers between devices  33.6 us (9%)
  local copies, waits for them, and re-layouts  20.5 us (6%)
  between operations  15.3 us (4%)
  matrix products  14.1 us (4%)
  other arithmetic  10.5 us (3%)
    all_gather x1, waiting for transfers between devices, attend(): lax.all_gather(short_vals, 'ctx', axis=0, tiled=True)  84.1 us
    all_gather x1, waiting for transfers between devices, attend(): lax.all_gather(short_keys, 'ctx', axis=0, tiled=True)  82.2 us
    psum x1, waiting for transfers between devices, shards(): lax.psum(grad_a.astype(jnp.bfloat16), 'dp').astype(jnp.float32)  71.4 us
    all_to_all x1, waiting for transfers between devices, shards(): lax.all_to_all(packed(attn), 'ctx', split_axis=0, concat_axis=0, tiled=True)  23.5 us
    all_to_all x1, starting transfers between devices, shards(): lax.all_to_all(packed(dy), 'ctx', split_axis=0, concat_axis=0, tiled=True)  16.9 us
    all_to_all x1, starting transfers between devices, shards(): lax.all_to_all(packed(attn), 'ctx', split_axis=0, concat_axis=0, tiled=True)  9.51 us
  transfers between devices with their start and end apart: 6, of which 4 were waited for; matrix products, arithmetic and copies ran while one was open for 9% of the time, Pallas kernels for 0%

commit v1 on v0

--- a/solution.py
+++ b/solution.py
@@ -89,7 +89,9 @@
     local = jnp.arange(segment_length, dtype=jnp.int32)[None, :] <= position[:, None]
     state = absorb(state, query_matrix, keys, values, local)
     piece = (
-        lax.all_gather(short_keys, "ctx", axis=0, tiled=True),
+        jnp.concatenate(
+            lax.all_to_all(jnp.stack([short_keys] * lax.axis_size("ctx")), "ctx", 0, 0), axis=0
+        ),
         lax.all_gather(short_vals, "ctx", axis=0, tiled=True),
     )
     count = piece[0].shape[0]

time: 356 us -> 311 us (0.87)
  waiting for transfers between devices: 261 us -> 207 us
  starting transfers between devices: 33.6 us -> 43 us
    all_gather x1 -> x0, waiting for transfers between devices: 82.2 us -> none  [attend(): lax.all_gather(short_keys, 'ctx', axis=0, tiled=True)]
    all_to_all x0 -> x1, waiting for transfers between devices: none -> 46.4 us  [attend(): lax.all_to_all(jnp.stack([short_keys] * lax.axis_size('ctx')), 'ctx', 0, 0)]
    all_gather x1, waiting for transfers between devices: 84.1 us -> 64.7 us  [attend(): lax.all_gather(short_vals, 'ctx', axis=0, tiled=True)]
    all_to_all x0 -> x1, starting transfers between devices: none -> 16.9 us  [attend(): lax.all_to_all(jnp.stack([short_keys] * lax.axis_size('ctx')), 'ctx', 0, 0)]
    all_to_all x1, starting transfers between devices: 16.9 us -> 9.68 us  [shards(): lax.all_to_all(packed(dy), 'ctx', split_axis=0, concat_axis=0, tiled=True)]
  transfers between devices with their start and end apart: 6 -> 6, of which waited for: 4 -> 4; matrix products, arithmetic and copies ran while one was open for 9% -> 10% of each run, Pallas kernels for 0% -> 0%
where the time goes in v1:
time: 311 us; the launch traced here: 310 us
  waiting for transfers between devices  207 us (67%)
  starting transfers between devices  43 us (14%)
  local copies, waits for them, and re-layouts  20.5 us (7%)
  between operations  15.6 us (5%)
  matrix products  13 us (4%)
  other arithmetic  10.5 us (3%)
    psum x1, waiting for transfers between devices, shards(): lax.psum(grad_a.astype(jnp.bfloat16), 'dp').astype(jnp.float32)  71.4 us
    all_gather x1, waiting for transfers between devices, attend(): lax.all_gather(short_vals, 'ctx', axis=0, tiled=True)  64.7 us
    all_to_all x1, waiting for transfers between devices, attend(): lax.all_to_all(jnp.stack([short_keys] * lax.axis_size('ctx')), 'ctx', 0, 0)  46.4 us
    all_to_all x1, waiting for transfers between devices, shards(): lax.all_to_all(packed(attn), 'ctx', split_axis=0, concat_axis=0, tiled=True)  24.5 us
    all_to_all x1, starting transfers between devices, attend(): lax.all_to_all(jnp.stack([short_keys] * lax.axis_size('ctx')), 'ctx', 0, 0)  16.9 us
    all_to_all x1, starting transfers between devices, shards(): lax.all_to_all(packed(dy), 'ctx', split_axis=0, concat_axis=0, tiled=True)  9.68 us
    all_to_all x1, starting transfers between devices, shards(): lax.all_to_all(packed(attn), 'ctx', split_axis=0, concat_axis=0, tiled=True)  9.51 us
    all_to_all x1, starting transfers between devices, shards(): lax.all_to_all(d_rows.reshape(count, cap, model), 'ctx', split_axis=0, co...  6.85 us
  transfers between devices with their start and end apart: 6, of which 4 were waited for; matrix products, arithmetic and copies ran while one was open for 10% of the time, Pallas kernels for 0%

profile of v1, /device:TPU:8, one launch (start us, length us, event | category | flops | bytes accessed | tf_op | source)
XLA Modules:
  0.0 309.8 jit_solution(9793872628496878645)
XLA Ops:
  7.2 1.5 fusion.61
  8.7 1.3 fusion.19
  10.0 1.6 stack.3
  11.6 16.9 %all-to-all-start.1 = ((bf16[64,16,1024]{2,1,0:T(8,128)(2,1)}), bf16[64,16,1024]{2,1,0:T(8,128)(2,1)}, u32[]{:S(2)}, u32[]{:S(2)}) async-start(bf16[64,16,1024]{2,1,0:T(8,128)(2,1)} %stack.3), calls=%async_computation.1 | async-start | bytes 4194304 | tf_op jit(solution)/shard_map/all_to_all | solution.py:93
  31.8 1.5 reshape.199
  34.5 46.4 %all-to-all-done.1 = bf16[64,16,1024]{2,1,0:T(8,128)(2,1)} async-done(((bf16[64,16,1024]{2,1,0:T(8,128)(2,1)}), bf16[64,16,1024]{2,1,0:T(8,128)(2,1)}, u32[]{:S(2)}, u32[]{:S(2)}) %all-to-all-start.1) | async-done | bytes 2097184 | tf_op jit(solution)/shard_map/all_to_all | solution.py:93
  80.8 9.7 %all-to-all-start = ((bf16[64,2,4096]{2,1,0:T(2,128)(2,1)}), bf16[64,2,4096]{2,1,0:T(2,128)(2,1)S(1)}, u32[]{:S(2)}, u32[]{:S(2)}) async-start(bf16[64,2,4096]{2,1,0:T(2,128)(2,1)} %reshape.199), calls=%async_computation | async-start | bytes 2097152 | tf_op jit(solution)/shard_map/all_to_all | solution.py:146
  90.5 64.7 %all-gather.2.cloned.1.call-done = bf16[1024,1024]{1,0:T(8,128)(2,1)} async-done(((bf16[16,1024]{1,0:T(8,128)(2,1)}), bf16[1024,1024]{1,0:T(8,128)(2,1)}) %all-gather.2.cloned.1.call-update) | async-done | bytes 2097168 | tf_op jit(solution)/shard_map/all_gather | solution.py:95
  155.2 11.0 %while.14 = (s32[]{:T(128)}, f32[16,8,4]{0,2,1:T(4,128)S(1)}, f32[16,8,4]{0,2,1:T(4,128)S(1)}, f32[16,8,4,128]{3,0,2,1:T(8,128)S(1)}, pred[4,1,256]{2,1,0:T(4,12...) while((s32[]{:T(128)}, f32[16,8,4]{0,2,1:T(4,128)S(1)}, ...), condition=%wide.region_8.9_spmd, body=%wide.region_5.8_spmd.sunk | while | flops 68420608 | bytes 7505253 | solution.py:51
  157.9 1.3 constant_dynamic-slice_fusion.3
  160.7 1.3 constant_dynamic-slice_fusion.3
  167.0 1.5 reshape.208
  168.5 9.5 %all-to-all-start.2 = ((bf16[64,2,4096]{2,1,0:T(2,128)(2,1)}), bf16[64,2,4096]{2,1,0:T(2,128)(2,1)S(1)}, u32[]{:S(2)}, u32[]{:S(2)}) async-start(bf16[64,2,4096]{2,1,0:T(2,128)(2,1)} %reshape.208), calls=%async_computation.2 | async-start | bytes 2097152 | tf_op jit(solution)/shard_map/all_to_all | solution.py:145
  178.8 24.5 %all-to-all-done.2 = bf16[64,2,4096]{2,1,0:T(2,128)(2,1)S(1)} async-done(((bf16[64,2,4096]{2,1,0:T(2,128)(2,1)}), bf16[64,2,4096]{2,1,0:T(2,128)(2,1)S(1)}, u32[]{:S(2)}, u32[]{:S(2)}) %all-to-all-start.2) | async-done | bytes 1048608 | tf_op jit(solution)/shard_map/all_to_all | solution.py:145
  206.3 1.7 add_convert_fusion
  207.9 2.5 reshape.209
  210.5 6.8 %all-to-all-start.3 = ((bf16[64,2,4096]{2,1,0:T(2,128)(2,1)}), bf16[64,2,4096]{2,1,0:T(2,128)(2,1)}, u32[]{:S(2)}, u32[]{:S(2)}) async-start(bf16[64,2,4096]{2,1,0:T(2,128)(2,1)} %reshape.209), calls=%async_computation.3 | async-start | bytes 2097152 | tf_op jit(solution)/shard_map/all_to_all | solution.py:169
  217.4 2.4 multiply_convert_fusion
  219.8 2.3 convert_element_type.95
  223.1 2.8 fusion.13
  225.9 71.4 %all-reduce.3.cloned.1.call-done = (bf16[1,16,4096]{2,1,0:T(8,128)(2,1)}, bf16[1,16,4096]{2,1,0:T(8,128)(2,1)}) async-done(((bf16[1,16,4096]{2,1,0:T(8,128)(2,1)}, bf16[1,16,4096]{2,1,0:T(8,128)(2,1)}), (bf16[1,16,4096]{2,1,0:T(8,128)(2,1)}, bf16[1,16,4096]{2,1,0:T(8,128)(2,1)})) %all-reduce.3.cloned.1.call-update) | async-done | bytes 262160 | tf_op jit(solution)/shard_map/psum | solution.py:176
  297.3 1.6 broadcast_in_dim.108
  298.9 1.6 broadcast_in_dim.110
  300.5 1.5 reshape.210
  (97 shorter events, 17.7 us)
Async XLA Ops:
  7.2 197.9 %copy-start = (bf16[1,16,4096]{2,1,0:T(8,128)(2,1)S(1)}, bf16[1,16,4096]{2,1,0:T(8,128)(2,1)}, u32[]{:S(2)}) copy-start(bf16[1,16,4096]{2,1,0:T(8,128)(2,1)} %param.20) | copy-start | bytes 393220
  11.6 17.0 %copy-start.5 = (bf16[256,1024]{1,0:T(8,128)(2,1)S(1)}, bf16[256,1024]{1,0:T(8,128)(2,1)}, u32[]{:S(2)}) copy-start(bf16[256,1024]{1,0:T(8,128)(2,1)} %param.14) | copy-start | bytes 1572868
  11.6 18.5 %copy-start.7 = (bf16[16,4096]{1,0:T(8,128)(2,1)S(1)}, bf16[16,4096]{1,0:T(8,128)(2,1)}, u32[]{:S(2)}) copy-start(bf16[16,4096]{1,0:T(8,128)(2,1)} %param.12) | copy-start | bytes 393220
  11.6 18.6 %copy-start.4 = (bf16[256,1024]{1,0:T(8,128)(2,1)S(1)}, bf16[256,1024]{1,0:T(8,128)(2,1)}, u32[]{:S(2)}) copy-start(bf16[256,1024]{1,0:T(8,128)(2,1)} %param.13) | copy-start | bytes 1572868
  11.6 69.2 %all-to-all-start.1 = ((bf16[64,16,1024]{2,1,0:T(8,128)(2,1)}), bf16[64,16,1024]{2,1,0:T(8,128)(2,1)}, u32[]{:S(2)}, u32[]{:S(2)}) async-start(bf16[64,16,1024]{2,1,0:T(8,128)(2,1)} %stack.3), calls=%async_computation.1 | async-start | bytes 4194304 | tf_op jit(solution)/shard_map/all_to_all | solution.py:93
  28.5 2.7 copy-start.9
  28.5 2.8 copy-start.8
  28.5 126.7 %all-gather.2.cloned.1.call-start = ((), (), s32[]{:S(2)}) async-start(), calls=%async_computation.4 | async-start | bytes 2129920 | tf_op jit(solution)/shard_map/all_gather | solution.py:95
  80.8 87.6 %all-to-all-start = ((bf16[64,2,4096]{2,1,0:T(2,128)(2,1)}), bf16[64,2,4096]{2,1,0:T(2,128)(2,1)S(1)}, u32[]{:S(2)}, u32[]{:S(2)}) async-start(bf16[64,2,4096]{2,1,0:T(2,128)(2,1)} %reshape.199), calls=%async_computation | async-start | bytes 2097152 | tf_op jit(solution)/shard_map/all_to_all | solution.py:146
  168.5 10.0 %copy-start.6 = (bf16[1,16,4096]{2,1,0:T(8,128)(2,1)S(1)}, bf16[1,16,4096]{2,1,0:T(8,128)(2,1)}, u32[]{:S(2)}) copy-start(bf16[1,16,4096]{2,1,0:T(8,128)(2,1)} %param.21) | copy-start | bytes 393220
  168.5 34.9 %all-to-all-start.2 = ((bf16[64,2,4096]{2,1,0:T(2,128)(2,1)}), bf16[64,2,4096]{2,1,0:T(2,128)(2,1)S(1)}, u32[]{:S(2)}, u32[]{:S(2)}) async-start(bf16[64,2,4096]{2,1,0:T(2,128)(2,1)} %reshape.208), calls=%async_computation.2 | async-start | bytes 2097152 | tf_op jit(solution)/shard_map/all_to_all | solution.py:145
  178.4 26.1 %copy-start.1 = (bf16[128,4096]{1,0:T(8,128)(2,1)}, bf16[128,4096]{1,0:T(8,128)(2,1)S(1)}, u32[]{:S(2)}) copy-start(bf16[128,4096]{1,0:T(8,128)(2,1)S(1)} %reshape.200) | copy-start | bytes 3145732
  205.0 1.2 copy-start.2
  210.5 90.0 %all-to-all-start.3 = ((bf16[64,2,4096]{2,1,0:T(2,128)(2,1)}), bf16[64,2,4096]{2,1,0:T(2,128)(2,1)}, u32[]{:S(2)}, u32[]{:S(2)}) async-start(bf16[64,2,4096]{2,1,0:T(2,128)(2,1)} %reshape.209), calls=%async_computation.3 | async-start | bytes 2097152 | tf_op jit(solution)/shard_map/all_to_all | solution.py:169
  217.3 79.9 %all-reduce.3.cloned.1.call-start = ((), (), s32[]{:S(2)}) async-start(), calls=%async_computation.5 | async-start | bytes 524288 | tf_op jit(solution)/shard_map/psum | solution.py:176
  219.8 3.3 %copy-start.3 = (bf16[128,4096]{1,0:T(8,128)(2,1)S(1)}, bf16[128,4096]{1,0:T(8,128)(2,1)}, u32[]{:S(2)}) copy-start(bf16[128,4096]{1,0:T(8,128)(2,1)} %copy-done.1) | copy-start | bytes 3145732
Sparse Core Ops, SparseCore 0:
  32.9 122.1 all-gather.1
  226.0 71.1 all-reduce.2
